TPU v7x, 32 devices: a whole 2x2x4 slice. The times are simulated.
32 devices in a mesh: clus: 8 (over z, x), blk: 4 (over y, core).
Axes of the slice: x: 2, y: 2, z: 4, core: 2. Of those that a mesh axis runs over, the one named last changes fastest.
Arguments:
- adjoint: bfloat16 [32, 384, 3, 128], P('clus', 'blk'), may hold values from -6 to 6
- blocks: bfloat16 [192, 384, 3, 1152], P('clus', 'blk'), may hold values from -0.1875 to 0.1875
- row_cluster: int32 [192], P('clus'), may hold values from 0 to 3
- col_owner: int32 [192, 1], P('clus'), may hold values from 0 to 7; in each aligned block of 24 rows (0 to 23, 24 to 47, ...) at most 6 rows name the same one
- col_cluster: int32 [192], P('clus'), may hold values from 0 to 3
- tangent: float32 [32, 3, 3, 384], P('clus', None, None, 'blk'), may hold values from -5 to 5
Outputs:
- sensitivity: float32 [32, 384, 3, 128], P('clus', 'blk')
Inputs may be any that keep to these rules, and one draw needn't show every extreme that they name: `col_owner`: among the 24 pairs stored by one index of clus (aligned blocks of the list), at most 6 name one owner, a bound that some block reaches of them.
All inputs are finite; a program needn't handle non-finite values.
Results may differ from a plain program's by a relative error of at most 0.0003.
Values sent between devices are 32-bit elements; how exact they have to be, the bound alone decides.
No kernel may reach another device: no remote copies, remote signals or barrier semaphores. Data moves between devices by JAX's collectives and lax.ppermute only.
A program may use at most 192 MiB of HBM per device.

v0:
```python
import functools

import jax
import jax.numpy as jnp
from jax import lax
from jax.experimental import pallas as pl
from jax.experimental.pallas import tpu as pltpu
from jax.sharding import PartitionSpec as P


PLAN = ((9, '10b2'), (8, 'b102'), (10, 'b120'), (9, '0b12'))

EVENTS = ('couple', (2, 0), (0, None), (3, None), (1, 0), (2, None), (0, None), (3, None), (1, None), (2, None), (0, None), (3, None), (1, None), (0, None), (2, None), (1, None), (3, None))

PER = 2
PARTS = 1
VMEM_BYTES = 67043328


def bits_of(size):
    return size.bit_length() - 1


def cut_rows(rows):
    whole = sum(share for share, _ in PLAN)
    edges, total = [0], 0
    for share, _ in PLAN:
        total += share
        edges.append(rows // 8 * total // whole * 8)
    edges[-1] = rows
    return list(zip(edges[:-1], edges[1:]))


def route(order, blk_bits, clus_bits):
    steps = []
    for letter in order:
        if letter == "b":
            steps += [("blk", bit) for bit in range(1, blk_bits)]
        elif int(letter) < clus_bits:
            steps.append(("clus", int(letter)))
    named = [bit for axis, bit in steps if axis == "clus"]
    return steps + [("clus", bit) for bit in range(clus_bits) if bit not in named]


def couple_kernel(cuts, piece, halves, aliased, row_ref, side_ref, adjoint_ref, block_ref, *rest):
    outs, result_ref = rest[aliased:-1], rest[-1]
    per = block_ref.shape[0]
    first = pl.program_id(0) * per
    side = side_ref[0]
    for inner in range(per):
        lam = adjoint_ref[row_ref[first + inner]]
        result_ref[inner] = lax.dot_general(
            block_ref[inner], lam, (((0,), (0,)), ((), ())), preferred_element_type=jnp.float32
        )
        for index, (begin, end) in enumerate(cuts):
            for half in range(halves):
                away = pl.multiple_of((2 * half + 1 - side) * piece + begin, 8)
                home = pl.multiple_of((2 * half + side) * piece + begin, 8)
                outs[2 * index][half, inner] = result_ref[inner, pl.ds(away, end - begin), :]
                outs[2 * index + 1][half, inner] = result_ref[inner, pl.ds(home, end - begin), :]


def couple(adjoint, blocks, rows, side, cuts, early, piece, halves, part, held):
    pairs, depth, width = blocks.shape
    clus_dev, _, right = adjoint.shape
    count = rows.shape[0]
    per = next(n for n in (PER, 2, 1) if count % n == 0)
    jump = part * count // per
    shapes, specs, aliases, extra = [], [], {}, []
    for (begin, end), alone in zip(cuts, early):
        for _ in range(2):
            shape = (halves, count if alone else pairs, end - begin, right)
            if not alone and part > 0:
                aliases[4 + len(extra)] = len(shapes)
                extra.append(held[len(shapes)])
            shapes.append(jax.ShapeDtypeStruct(shape, jnp.float32))
            move = 0 if alone else jump
            specs.append(
                pl.BlockSpec(
                    (halves, per, end - begin, right),
                    lambda p, rows, side, move=move: (0, p + move, 0, 0),
                )
            )
    grant = VMEM_BYTES - blocks.size * blocks.dtype.itemsize * 15 // 16
    return pl.pallas_call(
        functools.partial(couple_kernel, cuts, piece, halves, len(extra)),
        out_shape=shapes,
        grid_spec=pltpu.PrefetchScalarGridSpec(
            num_scalar_prefetch=2,
            grid=(count // per,),
            in_specs=[
                pl.BlockSpec((clus_dev, depth, right), lambda p, rows, side: (0, 0, 0)),
                pl.BlockSpec((per, depth, width), lambda p, rows, side: (p + jump, 0, 0)),
            ]
            + [pl.BlockSpec(memory_space=pl.ANY)] * len(extra),
            out_specs=specs,
            scratch_shapes=[pltpu.VMEM((per, width, right), jnp.float32)],
        ),
        input_output_aliases=aliases,
        name="couple",
        compiler_params=pltpu.CompilerParams(vmem_limit_bytes=grant),
        cost_estimate=pl.CostEstimate(
            flops=2 * count * depth * width * right,
            bytes_accessed=count * width * (2 * depth + 4 * right),
            transcendentals=0,
        ),
    )(rows, side, adjoint, blocks, *extra)


def gather_kernel(parts, slot_ref, *rest):
    values, (send_ref, home_ref, total_ref) = rest[: 2 * parts], rest[2 * parts :]
    total_ref[...] = jnp.zeros_like(total_ref)
    for part in range(parts):
        keep_ref, recv_ref = values[2 * part], values[2 * part + 1]
        count = keep_ref.shape[1]

        def add(pair, carry):
            slot = slot_ref[part * count + pair]
            total_ref[slot] += keep_ref[0, pair] + recv_ref[0, pair]
            return carry

        lax.fori_loop(0, count, add, 0, unroll=4)
    half = send_ref.shape[1]
    send_ref[0] = total_ref[:half]
    home_ref[0] = total_ref[half:]


def row_step(rows):
    best = 8
    for step in range(8, min(rows, 96) + 1, 8):
        if rows % step == 0:
            best = step
    return best


def gather_slots(slots, values, half):
    lead, count, rows, right = values[0].shape
    pairs = slots.shape[0]
    step = row_step(rows)
    shape = jax.ShapeDtypeStruct((lead, half, rows, right), jnp.float32)
    read = pl.BlockSpec((1, count, step, right), lambda a, r, s: (a, 0, r, 0))
    write = pl.BlockSpec((1, half, step, right), lambda a, r, s: (a, 0, r, 0))
    grant = 16 * step * right * (2 * pairs + 3 * half) + (2 << 20)
    return pl.pallas_call(
        functools.partial(gather_kernel, len(values) // 2),
        out_shape=[shape, shape],
        grid_spec=pltpu.PrefetchScalarGridSpec(
            num_scalar_prefetch=1,
            grid=(lead, rows // step),
            in_specs=[read] * len(values),
            out_specs=[write, write],
            scratch_shapes=[pltpu.VMEM((2 * half, step, right), jnp.float32)],
        ),
        name="gather_slots",
        compiler_params=pltpu.CompilerParams(vmem_limit_bytes=grant),
        cost_estimate=pl.CostEstimate(
            flops=2 * lead * pairs * rows * right,
            bytes_accessed=8 * lead * (pairs + half) * rows * right,
            transcendentals=0,
        ),
    )(slots, *values)


def finish_kernel(cuts, tangent_ref, *rest):
    parts, out_ref, field_ref = rest[:-2], rest[-2], rest[-1]
    for index, (begin, end) in enumerate(cuts):
        field_ref[begin:end] = parts[2 * index][0] + parts[2 * index + 1][0]
    tiles = out_ref.shape[2]
    field = [field_ref[pl.ds(comp, tiles, stride=3), :] for comp in range(3)]
    for out_comp in range(3):
        accum = tangent_ref[0, :, out_comp : out_comp + 1] * field[0]
        for in_comp in range(1, 3):
            place = 3 * in_comp + out_comp
            accum = accum + tangent_ref[0, :, place : place + 1] * field[in_comp]
        out_ref[0, out_comp] = accum


def finish(tangent, parts, cuts, piece):
    clus_dev, tiles, nine = tangent.shape
    right = parts[0].shape[-1]
    specs = [pl.BlockSpec((1, tiles, nine), lambda c: (c, 0, 0))]
    for part in parts:
        specs.append(pl.BlockSpec((1, part.shape[1], right), lambda c: (c, 0, 0)))
    return pl.pallas_call(
        functools.partial(finish_kernel, cuts),
        out_shape=jax.ShapeDtypeStruct((clus_dev, 3, tiles, right), jnp.float32),
        grid=(clus_dev,),
        in_specs=specs,
        out_specs=pl.BlockSpec((1, 3, tiles, right), lambda c: (c, 0, 0, 0)),
        scratch_shapes=[pltpu.VMEM((piece, right), jnp.float32)],
        name="finish",
        compiler_params=pltpu.CompilerParams(vmem_limit_bytes=8 << 20),
        cost_estimate=pl.CostEstimate(
            flops=18 * clus_dev * tiles * right,
            bytes_accessed=48 * clus_dev * tiles * right,
            transcendentals=0,
        ),
    )(tangent, *parts)


def local(adjoint, blocks, row_cluster, col_owner, col_cluster, tangent):
    pairs, tiles, comps, width = blocks.shape
    clus_dev, right = adjoint.shape[0], adjoint.shape[3]
    sizes = {"clus": lax.axis_size("clus"), "blk": lax.axis_size("blk")}
    here = {"clus": lax.axis_index("clus"), "blk": lax.axis_index("blk")}
    clus_bits, blk_bits = bits_of(sizes["clus"]), bits_of(sizes["blk"])
    piece = width // sizes["blk"]
    halves = sizes["blk"] // 2
    cuts = cut_rows(piece)
    owner = col_owner[:, 0]

    def my_bit(axis, bit):
        return (here[axis] >> bit) & 1

    def swap(value, axis, bit):
        return lax.ppermute(value, axis, [(i, i ^ (1 << bit)) for i in range(sizes[axis])])

    flat_adjoint = adjoint.transpose(0, 2, 1, 3).reshape(clus_dev, comps * tiles, right)
    flat_blocks = blocks.transpose(0, 2, 1, 3).reshape(pairs, comps * tiles, width)
    side = my_bit("blk", 0).astype(jnp.int32).reshape(1)
    half = sizes["clus"] * clus_dev // 2
    routes = [route(order, blk_bits, clus_bits) for _, order in PLAN]
    early = [steps[0][0] == "blk" for steps in routes]
    parts = next(n for n in (PARTS, 2, 1) if pairs % n == 0)
    count = pairs // parts

    def slots_for(bit):
        apart = (owner >> bit) & 1
        other = ((owner >> (bit + 1)) << bit) | (owner & ((1 << bit) - 1))
        home = (apart == my_bit("clus", bit)).astype(jnp.int32)
        return home * half + other * clus_dev + col_cluster

    def split(keep, recv, lead, axis, bit):
        rows = keep.shape[-2]
        both = [v.reshape(lead, 2, -1, rows, right) for v in (keep, recv)]
        mine = my_bit(axis, bit)

        def pick(which):
            left, other = (lax.dynamic_index_in_dim(v, which, 1, keepdims=False) for v in both)
            return left + other

        send, home = pick(1 - mine), pick(mine)
        recv = swap(send, axis, bit)
        return home, recv.reshape(home.shape)

    state = [None] * len(PLAN)
    used = [event[0] for event in EVENTS if event != "couple"]
    first_use = sorted(range(len(PLAN)), key=lambda c: used.index(c) if c in used else len(used))
    held = None

    def run_couple(part):
        nonlocal held
        rows = lax.slice_in_dim(row_cluster, part * count, (part + 1) * count)
        held = couple(flat_adjoint, flat_blocks, rows, side, cuts, early, piece, halves, part, held)
        for chunk in first_use:
            send, keep = held[2 * chunk], held[2 * chunk + 1]
            if early[chunk] or part == parts - 1:
                recv = swap(send, "blk", 0)
                state[chunk] = (state[chunk] or []) + [(keep, recv)]

    labels = [[("blk", bit) for bit in range(blk_bits - 1, 0, -1)] + ["pairs"] for _ in PLAN]
    done = {}

    def run(chunk, part=None):
        place = done.get((chunk, part), done.get((chunk, None), 0))
        if part is not None and (
            (chunk, part) in done or "pairs" not in labels[chunk] or part >= len(state[chunk])
        ):
            return
        if place >= len(routes[chunk]):
            return
        axis, bit = routes[chunk][place]
        if axis == "clus" and "pairs" in labels[chunk]:
            values = []
            for pair in state[chunk]:
                values += [v.reshape(-1, *v.shape[-3:]) for v in pair]
            slots = slots_for(bit)
            send, home = gather_slots(slots, values, half)
            recv = swap(send, axis, bit)
            labels[chunk] = labels[chunk][:-1] + [
                ("clus", b) for b in range(clus_bits - 1, -1, -1) if b != bit
            ] + ["own"]
            state[chunk] = [(home, recv)]
        else:
            spot = labels[chunk].index((axis, bit))
            which = range(len(state[chunk])) if part is None else [part]
            for index in which:
                if (chunk, index) in done and part is None and "pairs" in labels[chunk]:
                    continue
                state[chunk][index] = split(*state[chunk][index], 2**spot, axis, bit)
                if "pairs" in labels[chunk]:
                    done[(chunk, index)] = place + 1
            if "pairs" in labels[chunk] and len(
                [i for i in range(len(state[chunk])) if done.get((chunk, i)) == place + 1]
            ) < len(state[chunk]):
                return
            for index in range(len(state[chunk])):
                done.pop((chunk, index), None)
            labels[chunk] = labels[chunk][:spot] + labels[chunk][spot + 1 :]
        done[(chunk, None)] = place + 1

    ran = 0
    for event in EVENTS:
        if event == "couple":
            if ran < parts:
                run_couple(ran)
                ran += 1
        elif ran == parts or (event[1] is not None and event[1] < ran):
            run(*event)
    while ran < parts:
        run_couple(ran)
        ran += 1
    for _ in range(2 * clus_bits + 2 * blk_bits + 2 * parts):
        for chunk in range(len(PLAN)):
            run(chunk)
    parts = []
    for ((keep, recv),) in state:
        parts += [v.reshape(clus_dev, -1, right) for v in (keep, recv)]
    turned = tangent.transpose(0, 3, 1, 2).reshape(clus_dev, tiles, 9)
    out = finish(turned, parts, cuts, piece)
    return out.transpose(0, 2, 1, 3)


def solution(mesh):
    placed = (
        P("clus", "blk", None, None),
        P("clus", "blk", None, None),
        P("clus"),
        P("clus", None),
        P("clus"),
        P("clus", None, None, "blk"),
    )
    return jax.shard_map(
        local, mesh=mesh, in_specs=placed, out_specs=P("clus", "blk", None, None), check_vma=False
    )
```

profile of v0, /device:TPU:6, one launch (start us, length us, event | category | flops | bytes accessed | tf_op | source)
XLA Modules:
  0.0 131.8 jit_solution(3140034944708095599)
XLA Ops:
  1.6 17.1 %couple.1 = (f32[2,24,72,128]{3,2,1,0:T(8,128)}, f32[2,24,72,128]{3,2,1,0:T(8,128)}, f32[2,24,64,128]{3,2,1,0:T(8,128)}, f32[2,24,64,128]{3,2,1,0:T(8,128)S(1)},...) custom-call(s32[24]{0:T(128)S(1)} %copy-done.11, ...), custom_call_target="tpu_custom_call" | custom-call | flops 2038431744 | bytes 30081024 | tf_op jit(solution)/shard_map/couple/pallas_call | solution.py:85
  20.9 2.9 %collective-permute-done.rest_1_ = f32[2,24,72,128]{3,2,1,0:T(8,128)S(1)} collective-permute-done((f32[2,24,72,128]{3,2,1,0:T(8,128)}, f32[2,24,72,128]{3,2,1,0:T(8,128)S(1)}, u32[]{:S(2)}, u32[]{:S(2)}) %collective-permute-start) | collective-permute-done | bytes 1769504 | tf_op jit(solution)/shard_map/ppermute | solution.py:216
  23.7 1.5 %copy-done.1 = f32[2,24,72,128]{3,2,1,0:T(8,128)S(1)} copy-done((f32[2,24,72,128]{3,2,1,0:T(8,128)S(1)}, f32[2,24,72,128]{3,2,1,0:T(8,128)}, u32[]{:S(2)}) %copy-start.1) | copy-done | bytes 1769496
  25.2 2.0 %gather_slots.4 = (f32[2,16,72,128]{3,2,1,0:T(8,128)}, f32[2,16,72,128]{3,2,1,0:T(8,128)S(1)}) custom-call(s32[24]{0:T(128)S(1)} %get-tuple-element.58.slot_ref, f32[2,24,72,128]{3,2,1,0:T(8,128)S(1)} %copy-done.1, f32[2,24,72,128]{3,2,1,0:T(8,128)S(1)} %collective-permute-done.rest_1_), custom_call_target="tpu_custom_call" | custom-call | flops 884736 | bytes 5898240 | tf_op jit(solution)/shard_map/gather_slots/pallas_call | solution.py:144
  28.3 1.6 %collective-permute-start.1 = (f32[2,16,72,128]{3,2,1,0:T(8,128)}, f32[2,16,72,128]{3,2,1,0:T(8,128)}, u32[]{:S(2)}, u32[]{:S(2)}) collective-permute-start(f32[2,16,72,128]{3,2,1,0:T(8,128)} %get-tuple-element.24), channel_id=1, source_target_pairs={{0,8},{4,12},{8,0},{12,4},{16,24},{20,28},{24,16},{28,20},{1,9},{5... | collective-permute-start | bytes 3538952 | tf_op jit(solution)/shard_map/ppermute | solution.py:216
  29.9 2.0 %gather_slots.7 = (f32[2,16,72,128]{3,2,1,0:T(8,128)}, f32[2,16,72,128]{3,2,1,0:T(8,128)S(1)}) custom-call(s32[24]{0:T(128)S(1)} %get-tuple-element.57.slot_ref, f32[2,24,72,128]{3,2,1,0:T(8,128)S(1)} %copy-done, f32[2,24,72,128]{3,2,1,0:T(8,128)S(1)} %collective-permute-done.15.rest_1_), custom_call_target="tpu_custom_call" | custom-call | flops 884736 | bytes 5898240 | tf_op jit(solution)/shard_map/gather_slots/pallas_call | solution.py:144
  33.5 1.8 %dynamic-slice_add_fusion.2 = (f32[1,24,64,128]{3,2,1,0:T(8,128)S(1)}, f32[1,24,64,128]{3,2,1,0:T(8,128)S(1)}) fusion(f32[2,24,64,128]{3,2,1,0:T(8,128)} %collective-permute-done.5, s32[]{:T(128)S(6)} %select_n.79, f32[2,24,64,128]{3,2,1,0:T(8,128)S(1)} %copy-done.3, s32[]{:T(128)S(6)} %select_n.76), kind=kLoop, calls=%fused_computation.2 | loop fusion | flops 393216 | bytes 4718600 | tf_op jit(solution)/shard_map/add | solution.py:240
  35.9 2.7 %dynamic-slice_add_fusion = (f32[1,24,80,128]{3,2,1,0:T(8,128)}, f32[1,24,80,128]{3,2,1,0:T(8,128)S(1)}) fusion(f32[2,24,80,128]{3,2,1,0:T(8,128)} %collective-permute-done.10, s32[]{:T(128)S(6)} %select_n.79, f32[2,24,80,128]{3,2,1,0:T(8,128)S(1)} %copy-done.14, s32[]{:T(128)S(6)} %select_n.76), kind=kLoop, calls=%fused_computation | loop fusion | flops 491520 | bytes 5898248 | tf_op jit(solution)/shard_map/add | solution.py:240
  38.6 1.5 %collective-permute-start.11 = (f32[1,24,80,128]{3,2,1,0:T(8,128)}, f32[1,24,80,128]{3,2,1,0:T(8,128)S(1)}, u32[]{:S(2)}, u32[]{:S(2)}) collective-permute-start(f32[1,24,80,128]{3,2,1,0:T(8,128)} %get-tuple-element.37), channel_id=1, source_target_pairs={{0,2},{1,3},{2,0},{3,1},{4,6},{5,7},{6,4},{7,5},{8,10},{9,11},{10,... | collective-permute-start | bytes 2949128 | tf_op jit(solution)/shard_map/ppermute | solution.py:216
  40.1 15.7 %collective-permute-done.6.rest_1_ = f32[1,24,64,128]{3,2,1,0:T(8,128)S(1)} collective-permute-done((f32[1,24,64,128]{3,2,1,0:T(8,128)S(1)}, f32[1,24,64,128]{3,2,1,0:T(8,128)S(1)}, u32[]{:S(2)}, u32[]{:S(2)}) %collective-permute-start.6) | collective-permute-done | bytes 786464 | tf_op jit(solution)/shard_map/ppermute | solution.py:216
  55.8 1.6 %gather_slots.5 = (f32[1,16,64,128]{3,2,1,0:T(8,128)}, f32[1,16,64,128]{3,2,1,0:T(8,128)S(1)}) custom-call(s32[24]{0:T(128)S(1)} %get-tuple-element.58.slot_ref, f32[1,24,64,128]{3,2,1,0:T(8,128)S(1)} %get-tuple-element.40.rest_0_, f32[1,24,64,128]{3,2,1,0:T(8,128)S(1)} %collective-permute-done.6.rest_1_), custom_call_target="tpu_custom_call" | custom-call | flops 393216 | bytes 2621440 | tf_op jit(solution)/shard_map/gather_slots/pallas_call | solution.py:144
  58.6 2.5 %dynamic-slice_add_fusion.6 = (f32[4,1,4,72,128]{4,3,2,1,0:T(8,128)}, f32[4,4,72,128]{3,2,1,0:T(8,128)}) fusion(f32[4,2,4,72,128]{4,3,2,1,0:T(8,128)} %bitcast.9, s32[]{:T(128)S(6)} %select_n.75, f32[4,2,4,72,128]{4,3,2,1,0:T(8,128)S(1)} %bitcast.79, s32[]{:T(128)S(6)} %select_n.77), kind=kLoop, calls=%fused_computation.7 | loop fusion | flops 294912 | bytes 3538952 | tf_op jit(solution)/shard_map/add | solution.py:240
  61.1 1.5 %collective-permute-start.2 = (f32[4,4,72,128]{3,2,1,0:T(8,128)}, f32[4,4,72,128]{3,2,1,0:T(8,128)}, u32[]{:S(2)}, u32[]{:S(2)}) collective-permute-start(f32[4,4,72,128]{3,2,1,0:T(8,128)} %get-tuple-element.44), channel_id=1, source_target_pairs={{0,4},{4,0},{8,12},{12,8},{16,20},{20,16},{24,28},{28,24},{1,5},{5... | collective-permute-start | bytes 1769480 | tf_op jit(solution)/shard_map/ppermute | solution.py:216
  62.6 2.4 %dynamic-slice_add_fusion.5 = (f32[1,16,72,128]{3,2,1,0:T(8,128)}, f32[1,16,72,128]{3,2,1,0:T(8,128)}) fusion(f32[2,16,72,128]{3,2,1,0:T(8,128)} %collective-permute-done.16, s32[]{:T(128)S(6)} %select_n.76, f32[2,16,72,128]{3,2,1,0:T(8,128)S(1)} %copy-done.7, s32[]{:T(128)S(6)} %select_n.79), kind=kLoop, calls=%fused_computation.5 | loop fusion | flops 294912 | bytes 3538952 | tf_op jit(solution)/shard_map/add | solution.py:240
  65.5 11.3 %collective-permute-done.11.rest_1_ = f32[1,24,80,128]{3,2,1,0:T(8,128)S(1)} collective-permute-done((f32[1,24,80,128]{3,2,1,0:T(8,128)}, f32[1,24,80,128]{3,2,1,0:T(8,128)S(1)}, u32[]{:S(2)}, u32[]{:S(2)}) %collective-permute-start.11) | collective-permute-done | bytes 983072 | tf_op jit(solution)/shard_map/ppermute | solution.py:216
  76.8 1.7 %gather_slots.6 = (f32[1,16,80,128]{3,2,1,0:T(8,128)}, f32[1,16,80,128]{3,2,1,0:T(8,128)S(1)}) custom-call(s32[24]{0:T(128)S(1)} %get-tuple-element.58.slot_ref, f32[1,24,80,128]{3,2,1,0:T(8,128)S(1)} %get-tuple-element.38.rest_0_, f32[1,24,80,128]{3,2,1,0:T(8,128)S(1)} %collective-permute-done.11.rest_1_), custom_call_target="tpu_custom_call" | custom-call | flops 491520 | bytes 3276800 | tf_op jit(solution)/shard_map/gather_slots/pallas_call | solution.py:144
  80.0 1.5 %collective-permute-start.8 = (f32[2,4,64,128]{3,2,1,0:T(8,128)S(1)}, f32[2,4,64,128]{3,2,1,0:T(8,128)S(1)}, u32[]{:S(2)}, u32[]{:S(2)}) collective-permute-start(f32[2,4,64,128]{3,2,1,0:T(8,128)S(1)} %fusion.1), channel_id=1, source_target_pairs={{0,4},{4,0},{8,12},{12,8},{16,20},{20,16},{24,28},{28,24},{1,5},{5... | collective-permute-start | bytes 786440 | tf_op jit(solution)/shard_map/ppermute | solution.py:216
  84.3 5.3 %collective-permute-done.17 = f32[1,16,72,128]{3,2,1,0:T(8,128)} collective-permute-done((f32[1,16,72,128]{3,2,1,0:T(8,128)}, f32[1,16,72,128]{3,2,1,0:T(8,128)}, u32[]{:S(2)}, u32[]{:S(2)}) %collective-permute-start.17) | collective-permute-done | bytes 589856 | tf_op jit(solution)/shard_map/ppermute | solution.py:216
  91.1 8.9 %collective-permute-done.12 = f32[1,16,80,128]{3,2,1,0:T(8,128)S(1)} collective-permute-done((f32[1,16,80,128]{3,2,1,0:T(8,128)}, f32[1,16,80,128]{3,2,1,0:T(8,128)S(1)}, u32[]{:S(2)}, u32[]{:S(2)}) %collective-permute-start.12) | collective-permute-done | bytes 655392 | tf_op jit(solution)/shard_map/ppermute | solution.py:216
  101.8 2.3 %collective-permute-start.4 = (f32[1,4,72,128]{3,2,1,0:T(8,128)S(1)}, f32[1,4,72,128]{3,2,1,0:T(8,128)S(1)}, u32[]{:S(2)}, u32[]{:S(2)}) collective-permute-start(f32[1,4,72,128]{3,2,1,0:T(8,128)S(1)} %get-tuple-element.53), channel_id=1, source_target_pairs={{0,16},{4,20},{8,24},{12,28},{16,0},{20,4},{24,8},{28,12},{1,17},{... | collective-permute-start | bytes 442376 | tf_op jit(solution)/shard_map/ppermute | solution.py:216
  104.9 17.4 %collective-permute-done.13 = f32[1,8,80,128]{3,2,1,0:T(8,128)S(1)} collective-permute-done((f32[1,8,80,128]{3,2,1,0:T(8,128)S(1)}, f32[1,8,80,128]{3,2,1,0:T(8,128)S(1)}, u32[]{:S(2)}, u32[]{:S(2)}) %collective-permute-start.13) | collective-permute-done | bytes 327712 | tf_op jit(solution)/shard_map/ppermute | solution.py:216
  122.3 1.6 %collective-permute-start.14 = (f32[1,4,80,128]{3,2,1,0:T(8,128)S(1)}, f32[1,4,80,128]{3,2,1,0:T(8,128)S(1)}, u32[]{:S(2)}, u32[]{:S(2)}) collective-permute-start(f32[1,4,80,128]{3,2,1,0:T(8,128)S(1)} %get-tuple-element.49), channel_id=1, source_target_pairs={{0,4},{4,0},{8,12},{12,8},{16,20},{20,16},{24,28},{28,24},{1,5},{5... | collective-permute-start | bytes 491528 | tf_op jit(solution)/shard_map/ppermute | solution.py:216
  124.2 5.7 %collective-permute-done.9 = f32[1,4,64,128]{3,2,1,0:T(8,128)S(1)} collective-permute-done((f32[1,4,64,128]{3,2,1,0:T(8,128)S(1)}, f32[1,4,64,128]{3,2,1,0:T(8,128)S(1)}, u32[]{:S(2)}, u32[]{:S(2)}) %collective-permute-start.9) | collective-permute-done | bytes 131104 | tf_op jit(solution)/shard_map/ppermute | solution.py:216
  129.9 2.0 %finish.1 = f32[4,3,96,128]{3,2,1,0:T(8,128)} custom-call(f32[4,96,9]{2,1,0:T(8,128)S(1)} %copy.12.tangent_ref, f32[4,72,128]{2,1,0:T(8,128)S(1)} %get-tuple-element.54.rest_0_, f32[4,72,128]{2,1,0:T(8,128)S(1)} %bitcast.85, f32[4,64,128]{2,1,0:T(8,128)S(1)} %get-tuple-element.56.rest_2_, f32[4,64,128]{2,1,0:T(8,128)S(1)} %bitcast.87, ...), custom_call_target="tpu_custom_call" | custom-call | flops 884736 | bytes 2359296 | tf_op jit(solution)/shard_map/finish/pallas_call | solution.py:184
  (74 shorter events, 17.4 us)
Async XLA Ops:
  1.6 19.2 %copy-start.16 = (s32[24]{0:T(128)S(1)}, s32[24]{0:T(128)}, u32[]{:S(2)}) copy-start(s32[24]{0:T(128)} %param.10) | copy-start | bytes 292
  1.6 19.2 %copy-start.17 = (s32[24,1]{0,1:T(1,128)S(1)}, s32[24,1]{0,1:T(1,128)}, u32[]{:S(2)}) copy-start(s32[24,1]{0,1:T(1,128)} %param.9) | copy-start | bytes 292
  19.8 3.9 %collective-permute-start = (f32[2,24,72,128]{3,2,1,0:T(8,128)}, f32[2,24,72,128]{3,2,1,0:T(8,128)S(1)}, u32[]{:S(2)}, u32[]{:S(2)}) collective-permute-start(f32[2,24,72,128]{3,2,1,0:T(8,128)} %get-tuple-element.22), channel_id=1, source_target_pairs={{0,1},{1,0},{2,3},{3,2},{4,5},{5,4},{6,7},{7,6},{8,9},{9,8},{10,11... | collective-permute-start | bytes 5308424 | tf_op jit(solution)/shard_map/ppermute | solution.py:216
  19.8 10.1 %collective-permute-start.15 = (f32[2,24,72,128]{3,2,1,0:T(8,128)}, f32[2,24,72,128]{3,2,1,0:T(8,128)S(1)}, u32[]{:S(2)}, u32[]{:S(2)}) collective-permute-start(f32[2,24,72,128]{3,2,1,0:T(8,128)} %get-tuple-element.34), channel_id=1, source_target_pairs={{0,1},{1,0},{2,3},{3,2},{4,5},{5,4},{6,7},{7,6},{8,9},{9,8},{10,11... | collective-permute-start | bytes 5308424 | tf_op jit(solution)/shard_map/ppermute | solution.py:216
  20.3 15.5 %collective-permute-start.10 = (f32[2,24,80,128]{3,2,1,0:T(8,128)}, f32[2,24,80,128]{3,2,1,0:T(8,128)}, u32[]{:S(2)}, u32[]{:S(2)}) collective-permute-start(f32[2,24,80,128]{3,2,1,0:T(8,128)} %get-tuple-element.30), channel_id=1, source_target_pairs={{0,1},{1,0},{2,3},{3,2},{4,5},{5,4},{6,7},{7,6},{8,9},{9,8},{10,11... | collective-permute-start | bytes 5898248 | tf_op jit(solution)/shard_map/ppermute | solution.py:216
  20.3 13.2 %collective-permute-start.5 = (f32[2,24,64,128]{3,2,1,0:T(8,128)}, f32[2,24,64,128]{3,2,1,0:T(8,128)}, u32[]{:S(2)}, u32[]{:S(2)}) collective-permute-start(f32[2,24,64,128]{3,2,1,0:T(8,128)} %get-tuple-element.26), channel_id=1, source_target_pairs={{0,1},{1,0},{2,3},{3,2},{4,5},{5,4},{6,7},{7,6},{8,9},{9,8},{10,11... | collective-permute-start | bytes 4718600 | tf_op jit(solution)/shard_map/ppermute | solution.py:216
  28.3 30.3 %collective-permute-start.1 = (f32[2,16,72,128]{3,2,1,0:T(8,128)}, f32[2,16,72,128]{3,2,1,0:T(8,128)}, u32[]{:S(2)}, u32[]{:S(2)}) collective-permute-start(f32[2,16,72,128]{3,2,1,0:T(8,128)} %get-tuple-element.24), channel_id=1, source_target_pairs={{0,8},{4,12},{8,0},{12,4},{16,24},{20,28},{24,16},{28,20},{1,9},{5... | collective-permute-start | bytes 3538952 | tf_op jit(solution)/shard_map/ppermute | solution.py:216
  33.0 29.6 %collective-permute-start.16 = (f32[2,16,72,128]{3,2,1,0:T(8,128)}, f32[2,16,72,128]{3,2,1,0:T(8,128)}, u32[]{:S(2)}, u32[]{:S(2)}) collective-permute-start(f32[2,16,72,128]{3,2,1,0:T(8,128)} %get-tuple-element.36), channel_id=1, source_target_pairs={{0,4},{4,0},{8,12},{12,8},{16,20},{20,16},{24,28},{28,24},{1,5},{5... | collective-permute-start | bytes 3538952 | tf_op jit(solution)/shard_map/ppermute | solution.py:216
  35.3 20.5 %collective-permute-start.6 = (f32[1,24,64,128]{3,2,1,0:T(8,128)S(1)}, f32[1,24,64,128]{3,2,1,0:T(8,128)S(1)}, u32[]{:S(2)}, u32[]{:S(2)}) collective-permute-start(f32[1,24,64,128]{3,2,1,0:T(8,128)S(1)} %get-tuple-element.39), channel_id=1, source_target_pairs={{0,2},{1,3},{2,0},{3,1},{4,6},{5,7},{6,4},{7,5},{8,10},{9,11},{10,... | collective-permute-start | bytes 2359304 | tf_op jit(solution)/shard_map/ppermute | solution.py:216
  38.6 20.0 %copy-start.5 = (f32[2,16,72,128]{3,2,1,0:T(8,128)S(1)}, f32[2,16,72,128]{3,2,1,0:T(8,128)}, u32[]{:S(2)}) copy-start(f32[2,16,72,128]{3,2,1,0:T(8,128)} %copy-done.4) | copy-start | bytes 3538948
  38.6 38.3 %collective-permute-start.11 = (f32[1,24,80,128]{3,2,1,0:T(8,128)}, f32[1,24,80,128]{3,2,1,0:T(8,128)S(1)}, u32[]{:S(2)}, u32[]{:S(2)}) collective-permute-start(f32[1,24,80,128]{3,2,1,0:T(8,128)} %get-tuple-element.37), channel_id=1, source_target_pairs={{0,2},{1,3},{2,0},{3,1},{4,6},{5,7},{6,4},{7,5},{8,10},{9,11},{10,... | collective-permute-start | bytes 2949128 | tf_op jit(solution)/shard_map/ppermute | solution.py:216
  58.2 20.8 %collective-permute-start.7 = (f32[1,16,64,128]{3,2,1,0:T(8,128)}, f32[1,16,64,128]{3,2,1,0:T(8,128)}, u32[]{:S(2)}, u32[]{:S(2)}) collective-permute-start(f32[1,16,64,128]{3,2,1,0:T(8,128)} %get-tuple-element.28), channel_id=1, source_target_pairs={{0,8},{4,12},{8,0},{12,4},{16,24},{20,28},{24,16},{28,20},{1,9},{5... | collective-permute-start | bytes 1572872 | tf_op jit(solution)/shard_map/ppermute | solution.py:216
  61.1 21.5 %collective-permute-start.2 = (f32[4,4,72,128]{3,2,1,0:T(8,128)}, f32[4,4,72,128]{3,2,1,0:T(8,128)}, u32[]{:S(2)}, u32[]{:S(2)}) collective-permute-start(f32[4,4,72,128]{3,2,1,0:T(8,128)} %get-tuple-element.44), channel_id=1, source_target_pairs={{0,4},{4,0},{8,12},{12,8},{16,20},{20,16},{24,28},{28,24},{1,5},{5... | collective-permute-start | bytes 1769480 | tf_op jit(solution)/shard_map/ppermute | solution.py:216
  65.0 24.5 %collective-permute-start.17 = (f32[1,16,72,128]{3,2,1,0:T(8,128)}, f32[1,16,72,128]{3,2,1,0:T(8,128)}, u32[]{:S(2)}, u32[]{:S(2)}) collective-permute-start(f32[1,16,72,128]{3,2,1,0:T(8,128)} %get-tuple-element.42), channel_id=1, source_target_pairs={{0,2},{1,3},{2,0},{3,1},{4,6},{5,7},{6,4},{7,5},{8,10},{9,11},{10,... | collective-permute-start | bytes 1769480 | tf_op jit(solution)/shard_map/ppermute | solution.py:216
  78.5 21.4 %collective-permute-start.12 = (f32[1,16,80,128]{3,2,1,0:T(8,128)}, f32[1,16,80,128]{3,2,1,0:T(8,128)S(1)}, u32[]{:S(2)}, u32[]{:S(2)}) collective-permute-start(f32[1,16,80,128]{3,2,1,0:T(8,128)} %get-tuple-element.32), channel_id=1, source_target_pairs={{0,8},{4,12},{8,0},{12,4},{16,24},{20,28},{24,16},{28,20},{1,9},{5... | collective-permute-start | bytes 1966088 | tf_op jit(solution)/shard_map/ppermute | solution.py:216
  80.0 43.9 %collective-permute-start.8 = (f32[2,4,64,128]{3,2,1,0:T(8,128)S(1)}, f32[2,4,64,128]{3,2,1,0:T(8,128)S(1)}, u32[]{:S(2)}, u32[]{:S(2)}) collective-permute-start(f32[2,4,64,128]{3,2,1,0:T(8,128)S(1)} %fusion.1), channel_id=1, source_target_pairs={{0,4},{4,0},{8,12},{12,8},{16,20},{20,16},{24,28},{28,24},{1,5},{5... | collective-permute-start | bytes 786440 | tf_op jit(solution)/shard_map/ppermute | solution.py:216
  83.7 18.0 %collective-permute-start.3 = (f32[1,8,72,128]{3,2,1,0:T(8,128)S(1)}, f32[1,8,72,128]{3,2,1,0:T(8,128)S(1)}, u32[]{:S(2)}, u32[]{:S(2)}) collective-permute-start(f32[1,8,72,128]{3,2,1,0:T(8,128)S(1)} %get-tuple-element.48), channel_id=1, source_target_pairs={{0,2},{1,3},{2,0},{3,1},{4,6},{5,7},{6,4},{7,5},{8,10},{9,11},{10,... | collective-permute-start | bytes 884744 | tf_op jit(solution)/shard_map/ppermute | solution.py:216
  90.6 13.6 %collective-permute-start.18 = (f32[2,4,72,128]{3,2,1,0:T(8,128)S(1)}, f32[2,4,72,128]{3,2,1,0:T(8,128)S(1)}, u32[]{:S(2)}, u32[]{:S(2)}) collective-permute-start(f32[2,4,72,128]{3,2,1,0:T(8,128)S(1)} %fusion), channel_id=1, source_target_pairs={{0,8},{4,12},{8,0},{12,4},{16,24},{20,28},{24,16},{28,20},{1,9},{5... | collective-permute-start | bytes 884744 | tf_op jit(solution)/shard_map/ppermute | solution.py:216
  100.0 22.3 %collective-permute-start.13 = (f32[1,8,80,128]{3,2,1,0:T(8,128)S(1)}, f32[1,8,80,128]{3,2,1,0:T(8,128)S(1)}, u32[]{:S(2)}, u32[]{:S(2)}) collective-permute-start(f32[1,8,80,128]{3,2,1,0:T(8,128)S(1)} %get-tuple-element.46), channel_id=1, source_target_pairs={{0,16},{4,20},{8,24},{12,28},{16,0},{20,4},{24,8},{28,12},{1,17},{... | collective-permute-start | bytes 983048 | tf_op jit(solution)/shard_map/ppermute | solution.py:216
  101.8 22.3 %copy-start.15 = (f32[4,3,3,96]{3,0,2,1:T(4,128)S(1)}, f32[4,3,3,96]{3,0,2,1:T(4,128)}, u32[]{:S(2)}) copy-start(f32[4,3,3,96]{3,0,2,1:T(4,128)} %param.11) | copy-start | bytes 41476
  101.8 28.0 %collective-permute-start.4 = (f32[1,4,72,128]{3,2,1,0:T(8,128)S(1)}, f32[1,4,72,128]{3,2,1,0:T(8,128)S(1)}, u32[]{:S(2)}, u32[]{:S(2)}) collective-permute-start(f32[1,4,72,128]{3,2,1,0:T(8,128)S(1)} %get-tuple-element.53), channel_id=1, source_target_pairs={{0,16},{4,20},{8,24},{12,28},{16,0},{20,4},{24,8},{28,12},{1,17},{... | collective-permute-start | bytes 442376 | tf_op jit(solution)/shard_map/ppermute | solution.py:216
  104.2 25.7 %collective-permute-start.19 = (f32[1,4,72,128]{3,2,1,0:T(8,128)S(1)}, f32[1,4,72,128]{3,2,1,0:T(8,128)S(1)}, u32[]{:S(2)}, u32[]{:S(2)}) collective-permute-start(f32[1,4,72,128]{3,2,1,0:T(8,128)S(1)} %get-tuple-element.51), channel_id=1, source_target_pairs={{0,16},{4,20},{8,24},{12,28},{16,0},{20,4},{24,8},{28,12},{1,17},{... | collective-permute-start | bytes 442376 | tf_op jit(solution)/shard_map/ppermute | solution.py:216
  122.3 7.5 %collective-permute-start.14 = (f32[1,4,80,128]{3,2,1,0:T(8,128)S(1)}, f32[1,4,80,128]{3,2,1,0:T(8,128)S(1)}, u32[]{:S(2)}, u32[]{:S(2)}) collective-permute-start(f32[1,4,80,128]{3,2,1,0:T(8,128)S(1)} %get-tuple-element.49), channel_id=1, source_target_pairs={{0,4},{4,0},{8,12},{12,8},{16,20},{20,16},{24,28},{28,24},{1,5},{5... | collective-permute-start | bytes 491528 | tf_op jit(solution)/shard_map/ppermute | solution.py:216
  123.9 5.9 %collective-permute-start.9 = (f32[1,4,64,128]{3,2,1,0:T(8,128)S(1)}, f32[1,4,64,128]{3,2,1,0:T(8,128)S(1)}, u32[]{:S(2)}, u32[]{:S(2)}) collective-permute-start(f32[1,4,64,128]{3,2,1,0:T(8,128)S(1)} %get-tuple-element.55), channel_id=1, source_target_pairs={{0,16},{4,20},{8,24},{12,28},{16,0},{20,4},{24,8},{28,12},{1,17},{... | collective-permute-start | bytes 393224 | tf_op jit(solution)/shard_map/ppermute | solution.py:216
  (14 other events, 50.4 us)
where the time goes:
time: 134 us; the launch traced here: 132 us
  waiting for transfers between devices  67.1 us (50%)
  Pallas kernels  26.4 us (20%)
  starting transfers between devices  16.2 us (12%)
  other arithmetic  14.8 us (11%)
  local copies, waits for them, and re-layouts  7.29 us (5%)
    ppermute x20, waiting for transfers between devices, swap(): lax.ppermute(value, axis, [(i, i ^ 1 << bit) for i in range(sizes[axis])])  67.1 us
    pallas_call x1, Pallas kernels, couple(): pl.pallas_call(functools.partial(couple_kernel, cuts, piece, halves, len(...  17.1 us
    ppermute x20, starting transfers between devices, swap(): lax.ppermute(value, axis, [(i, i ^ 1 << bit) for i in range(sizes[axis])])  16.2 us
    add x14, other arithmetic, pick(): return left + other  14.8 us
    pallas_call x4, Pallas kernels, gather_slots(): pl.pallas_call(functools.partial(gather_kernel, len(values) // 2), out_sh...  7.35 us
    unnamed x36, local copies, waits for them, and re-layouts  7.17 us
  transfers between devices with their start and end apart: 20, of which 7 were waited for; matrix products, arithmetic and copies ran while one was open for 11% of the time, Pallas kernels for 6%

commit v1 on v0

--- a/solution.py
+++ b/solution.py
@@ -8,13 +8,12 @@
 from jax.sharding import PartitionSpec as P
 
 
-PLAN = ((9, '10b2'), (8, 'b102'), (10, 'b120'), (9, '0b12'))
-
-EVENTS = ('couple', (2, 0), (0, None), (3, None), (1, 0), (2, None), (0, None), (3, None), (1, None), (2, None), (0, None), (3, None), (1, None), (0, None), (2, None), (1, None), (3, None))
-
-PER = 2
+PLAN = ((10, 'b012'), (9, '1b02'), (8, 'b012'), (9, '012b'))
+
+EVENTS = ('couple', (2, 0), (3, None), (1, None), (0, 0), (2, None), (3, None), (1, None), (0, None), (2, None), (3, None), (1, None), (2, None), (0, None), (1, None), (3, None), (0, None))
+
+PER = 6
 PARTS = 1
-VMEM_BYTES = 67043328
 
 
 def bits_of(size):
@@ -50,8 +49,8 @@
     for inner in range(per):
         lam = adjoint_ref[row_ref[first + inner]]
         result_ref[inner] = lax.dot_general(
-            block_ref[inner], lam, (((0,), (0,)), ((), ())), preferred_element_type=jnp.float32
-        )
+            lam, block_ref[inner], (((0,), (0,)), ((), ())), preferred_element_type=jnp.float32
+        ).T
         for index, (begin, end) in enumerate(cuts):
             for half in range(halves):
                 away = pl.multiple_of((2 * half + 1 - side) * piece + begin, 8)
@@ -64,7 +63,7 @@
     pairs, depth, width = blocks.shape
     clus_dev, _, right = adjoint.shape
     count = rows.shape[0]
-    per = next(n for n in (PER, 2, 1) if count % n == 0)
+    per = next(n for n in (PER, 4, 3, 2, 1) if count % n == 0)
     jump = part * count // per
     shapes, specs, aliases, extra = [], [], {}, []
     for (begin, end), alone in zip(cuts, early):
@@ -73,7 +72,7 @@
             if not alone and part > 0:
                 aliases[4 + len(extra)] = len(shapes)
                 extra.append(held[len(shapes)])
-            shapes.append(jax.ShapeDtypeStruct(shape, jnp.float32))
+            shapes.append(pltpu.HBM(shape, jnp.float32))
             move = 0 if alone else jump
             specs.append(
                 pl.BlockSpec(
@@ -81,7 +80,7 @@
                     lambda p, rows, side, move=move: (0, p + move, 0, 0),
                 )
             )
-    grant = VMEM_BYTES - blocks.size * blocks.dtype.itemsize * 15 // 16
+    grant = 4 * per * width * (depth + 3 * right) + (3 << 20)
     return pl.pallas_call(
         functools.partial(couple_kernel, cuts, piece, halves, len(extra)),
         out_shape=shapes,
@@ -104,7 +103,13 @@
             bytes_accessed=count * width * (2 * depth + 4 * right),
             transcendentals=0,
         ),
-    )(rows, side, adjoint, blocks, *extra)
+    )(
+        pltpu.with_memory_space_constraint(rows, pltpu.HBM),
+        side,
+        pltpu.with_memory_space_constraint(adjoint, pltpu.HBM),
+        pltpu.with_memory_space_constraint(blocks, pltpu.HBM),
+        *extra,
+    )
 
 
 def gather_kernel(parts, slot_ref, *rest):

time: 134 us -> 128 us (0.955)
  waiting for transfers between devices: 67.1 us -> 59.8 us
  starting transfers between devices: 16.2 us -> 20.7 us
  Pallas kernels: 26.4 us -> 22.4 us
    ppermute x20, waiting for transfers between devices: 67.1 us -> 59.8 us  [swap(): lax.ppermute(value, axis, [(i, i ^ 1 << bit) for i in range(sizes[axis])])]
    ppermute x20, starting transfers between devices: 16.2 us -> 20.7 us  [swap(): lax.ppermute(value, axis, [(i, i ^ 1 << bit) for i in range(sizes[axis])])]
    pallas_call x1, Pallas kernels: 17.1 us -> 13.9 us  [couple(): pl.pallas_call(functools.partial(couple_kernel, cuts, piece, halves, len(...]
    add x14 -> x16, other arithmetic: 14.8 us -> 15.7 us  [pick(): return left + other]
    unnamed x36 -> x34, local copies, waits for them, and re-layouts: 7.17 us -> 7.23 us
  transfers between devices with their start and end apart: 20 -> 20, of which waited for: 7 -> 8; matrix products, arithmetic and copies ran while one was open for 11% -> 13% of each run, Pallas kernels for 6% -> 5%
where the time goes in v1:
time: 128 us; the launch traced here: 126 us
  waiting for transfers between devices  59.8 us (47%)
  Pallas kernels  22.4 us (18%)
  starting transfers between devices  20.7 us (16%)
  other arithmetic  15.7 us (12%)
  local copies, waits for them, and re-layouts  7.35 us (6%)
    ppermute x20, waiting for transfers between devices, swap(): lax.ppermute(value, axis, [(i, i ^ 1 << bit) for i in range(sizes[axis])])  59.8 us
    ppermute x20, starting transfers between devices, swap(): lax.ppermute(value, axis, [(i, i ^ 1 << bit) for i in range(sizes[axis])])  20.7 us
    add x16, other arithmetic, pick(): return left + other  15.7 us
    pallas_call x1, Pallas kernels, couple(): pl.pallas_call(functools.partial(couple_kernel, cuts, piece, halves, len(...  13.9 us
    unnamed x34, local copies, waits for them, and re-layouts  7.23 us
    pallas_call x4, Pallas kernels, gather_slots(): pl.pallas_call(functools.partial(gather_kernel, len(values) // 2), out_sh...  6.56 us
  transfers between devices with their start and end apart: 20, of which 8 were waited for; matrix products, arithmetic and copies ran while one was open for 13% of the time, Pallas kernels for 5%

profile of v1, /device:TPU:6, one launch (start us, length us, event | category | flops | bytes accessed | tf_op | source)
XLA Modules:
  0.0 126.1 jit_solution(11894433254854309145)
XLA Ops:
  0.0 13.9 %couple.1 = (f32[2,24,80,128]{3,2,1,0:T(8,128)}, f32[2,24,80,128]{3,2,1,0:T(8,128)}, f32[2,24,72,128]{3,2,1,0:T(8,128)}, f32[2,24,72,128]{3,2,1,0:T(8,128)}, f32...) custom-call(s32[24]{0:T(128)} %row_ref.1, ...), custom_call_target="tpu_custom_call" | custom-call | flops 2038431744 | bytes 30081024 | tf_op jit(solution)/shard_map/couple/pallas_call | solution.py:84
  14.9 2.9 %collective-permute-done.5.rest_1_ = f32[2,24,72,128]{3,2,1,0:T(8,128)S(1)} collective-permute-done((f32[2,24,72,128]{3,2,1,0:T(8,128)}, f32[2,24,72,128]{3,2,1,0:T(8,128)S(1)}, u32[]{:S(2)}, u32[]{:S(2)}) %collective-permute-start.5) | collective-permute-done | bytes 1769504 | tf_op jit(solution)/shard_map/ppermute | solution.py:221
  19.1 1.5 %copy-done.1 = f32[2,24,72,128]{3,2,1,0:T(8,128)S(1)} copy-done((f32[2,24,72,128]{3,2,1,0:T(8,128)S(1)}, f32[2,24,72,128]{3,2,1,0:T(8,128)}, u32[]{:S(2)}) %copy-start.1) | copy-done | bytes 1769496
  22.0 2.0 %gather_slots.5 = (f32[2,16,72,128]{3,2,1,0:T(8,128)}, f32[2,16,72,128]{3,2,1,0:T(8,128)S(1)}) custom-call(s32[24]{0:T(128)S(1)} %get-tuple-element.53.slot_ref, f32[2,24,72,128]{3,2,1,0:T(8,128)S(1)} %copy-done.1, f32[2,24,72,128]{3,2,1,0:T(8,128)S(1)} %copy-done.3), custom_call_target="tpu_custom_call" | custom-call | flops 884736 | bytes 5898240 | tf_op jit(solution)/shard_map/gather_slots/pallas_call | solution.py:149
  25.2 1.6 %collective-permute-start.6 = (f32[2,16,72,128]{3,2,1,0:T(8,128)}, f32[2,16,72,128]{3,2,1,0:T(8,128)}, u32[]{:S(2)}, u32[]{:S(2)}) collective-permute-start(f32[2,16,72,128]{3,2,1,0:T(8,128)} %get-tuple-element.28), channel_id=1, source_target_pairs={{0,8},{4,12},{8,0},{12,4},{16,24},{20,28},{24,16},{28,20},{1,9},{5... | collective-permute-start | bytes 3538952 | tf_op jit(solution)/shard_map/ppermute | solution.py:221
  26.7 2.1 %gather_slots.7 = (f32[2,16,72,128]{3,2,1,0:T(8,128)}, f32[2,16,72,128]{3,2,1,0:T(8,128)S(1)}) custom-call(s32[24]{0:T(128)S(1)} %get-tuple-element.54.slot_ref, f32[2,24,72,128]{3,2,1,0:T(8,128)S(1)} %copy-done, f32[2,24,72,128]{3,2,1,0:T(8,128)S(1)} %collective-permute-done.15.rest_1_), custom_call_target="tpu_custom_call" | custom-call | flops 884736 | bytes 5898240 | tf_op jit(solution)/shard_map/gather_slots/pallas_call | solution.py:149
  30.4 1.8 %dynamic-slice_add_fusion.2 = (f32[1,24,64,128]{3,2,1,0:T(8,128)S(1)}, f32[1,24,64,128]{3,2,1,0:T(8,128)S(1)}) fusion(f32[2,24,64,128]{3,2,1,0:T(8,128)} %collective-permute-done.10, s32[]{:T(128)S(6)} %select_n.75, f32[2,24,64,128]{3,2,1,0:T(8,128)S(1)} %copy-done.13, s32[]{:T(128)S(6)} %select_n.74), kind=kLoop, calls=%fused_computation.2 | loop fusion | flops 393216 | bytes 4718600 | tf_op jit(solution)/shard_map/add | solution.py:245
  32.7 2.7 %dynamic-slice_add_fusion = (f32[1,24,80,128]{3,2,1,0:T(8,128)}, f32[1,24,80,128]{3,2,1,0:T(8,128)S(1)}) fusion(f32[2,24,80,128]{3,2,1,0:T(8,128)} %collective-permute-done, s32[]{:T(128)S(6)} %select_n.75, f32[2,24,80,128]{3,2,1,0:T(8,128)S(1)} %copy-done.12, s32[]{:T(128)S(6)} %select_n.74), kind=kLoop, calls=%fused_computation | loop fusion | flops 491520 | bytes 5898248 | tf_op jit(solution)/shard_map/add | solution.py:245
  35.4 1.5 %collective-permute-start.1 = (f32[1,24,80,128]{3,2,1,0:T(8,128)}, f32[1,24,80,128]{3,2,1,0:T(8,128)S(1)}, u32[]{:S(2)}, u32[]{:S(2)}) collective-permute-start(f32[1,24,80,128]{3,2,1,0:T(8,128)} %get-tuple-element.37), channel_id=1, source_target_pairs={{0,2},{1,3},{2,0},{3,1},{4,6},{5,7},{6,4},{7,5},{8,10},{9,11},{10,... | collective-permute-start | bytes 2949128 | tf_op jit(solution)/shard_map/ppermute | solution.py:221
  37.0 15.7 %collective-permute-done.11.rest_1_ = f32[1,24,64,128]{3,2,1,0:T(8,128)S(1)} collective-permute-done((f32[1,24,64,128]{3,2,1,0:T(8,128)S(1)}, f32[1,24,64,128]{3,2,1,0:T(8,128)S(1)}, u32[]{:S(2)}, u32[]{:S(2)}) %collective-permute-start.11) | collective-permute-done | bytes 786464 | tf_op jit(solution)/shard_map/ppermute | solution.py:221
  52.7 1.6 %gather_slots.6 = (f32[1,16,64,128]{3,2,1,0:T(8,128)}, f32[1,16,64,128]{3,2,1,0:T(8,128)S(1)}) custom-call(s32[24]{0:T(128)S(1)} %get-tuple-element.54.slot_ref, f32[1,24,64,128]{3,2,1,0:T(8,128)S(1)} %get-tuple-element.40.rest_0_, f32[1,24,64,128]{3,2,1,0:T(8,128)S(1)} %collective-permute-done.11.rest_1_), custom_call_target="tpu_custom_call" | custom-call | flops 393216 | bytes 2621440 | tf_op jit(solution)/shard_map/gather_slots/pallas_call | solution.py:149
  55.1 1.5 %collective-permute-start.12 = (f32[1,16,64,128]{3,2,1,0:T(8,128)}, f32[1,16,64,128]{3,2,1,0:T(8,128)}, u32[]{:S(2)}, u32[]{:S(2)}) collective-permute-start(f32[1,16,64,128]{3,2,1,0:T(8,128)} %get-tuple-element.32), channel_id=1, source_target_pairs={{0,4},{4,0},{8,12},{12,8},{16,20},{20,16},{24,28},{28,24},{1,5},{5... | collective-permute-start | bytes 1572872 | tf_op jit(solution)/shard_map/ppermute | solution.py:221
  56.6 2.5 %dynamic-slice_add_fusion.5 = (f32[1,16,72,128]{3,2,1,0:T(8,128)}, f32[1,16,72,128]{3,2,1,0:T(8,128)}) fusion(f32[2,16,72,128]{3,2,1,0:T(8,128)} %collective-permute-done.6, s32[]{:T(128)S(6)} %select_n.74, f32[2,16,72,128]{3,2,1,0:T(8,128)S(1)} %copy-done.5, s32[]{:T(128)S(6)} %select_n.75), kind=kLoop, calls=%fused_computation.8 | loop fusion | flops 294912 | bytes 3538952 | tf_op jit(solution)/shard_map/add | solution.py:245
  59.6 2.4 %bitcast_add_fusion.1 = (f32[4,1,4,72,128]{4,3,2,0,1:T(8,128)}, f32[4,4,72,128]{3,2,1,0:T(8,128)}) fusion(f32[4,2,4,72,128]{4,3,2,1,0:T(8,128)} %bitcast.31, s32[]{:T(128)S(6)} %select_n.76, f32[4,2,4,72,128]{4,3,2,1,0:T(8,128)S(1)} %bitcast.105, s32[]{:T(128)S(6)} %select_n.78), kind=kLoop, calls=%fused_computation.6 | loop fusion | flops 294912 | bytes 3538952 | tf_op jit(solution)/shard_map/add | solution.py:245
  62.5 11.2 %collective-permute-done.1.rest_1_ = f32[1,24,80,128]{3,2,1,0:T(8,128)S(1)} collective-permute-done((f32[1,24,80,128]{3,2,1,0:T(8,128)}, f32[1,24,80,128]{3,2,1,0:T(8,128)S(1)}, u32[]{:S(2)}, u32[]{:S(2)}) %collective-permute-start.1) | collective-permute-done | bytes 983072 | tf_op jit(solution)/shard_map/ppermute | solution.py:221
  74.6 1.5 %collective-permute-start.2 = (f32[1,16,80,128]{3,2,1,0:T(8,128)S(1)}, f32[1,16,80,128]{3,2,1,0:T(8,128)S(1)}, u32[]{:S(2)}, u32[]{:S(2)}) collective-permute-start(f32[1,16,80,128]{3,2,1,0:T(8,128)S(1)} %get-tuple-element.24), channel_id=1, source_target_pairs={{0,4},{4,0},{8,12},{12,8},{16,20},{20,16},{24,28},{28,24},{1,5},{5... | collective-permute-start | bytes 1966088 | tf_op jit(solution)/shard_map/ppermute | solution.py:221
  78.7 6.4 %collective-permute-done.7 = f32[1,16,72,128]{3,2,1,0:T(8,128)} collective-permute-done((f32[1,16,72,128]{3,2,1,0:T(8,128)}, f32[1,16,72,128]{3,2,1,0:T(8,128)}, u32[]{:S(2)}, u32[]{:S(2)}) %collective-permute-start.7) | collective-permute-done | bytes 589856 | tf_op jit(solution)/shard_map/ppermute | solution.py:221
  86.1 1.5 %collective-permute-start.8 = (f32[2,4,72,128]{3,2,1,0:T(8,128)S(1)}, f32[2,4,72,128]{3,2,1,0:T(8,128)S(1)}, u32[]{:S(2)}, u32[]{:S(2)}) collective-permute-start(f32[2,4,72,128]{3,2,1,0:T(8,128)S(1)} %fusion.3), channel_id=1, source_target_pairs={{0,4},{4,0},{8,12},{12,8},{16,20},{20,16},{24,28},{28,24},{1,5},{5... | collective-permute-start | bytes 884744 | tf_op jit(solution)/shard_map/ppermute | solution.py:221
  90.7 2.7 %collective-permute-start.18 = (f32[2,4,72,128]{3,2,1,0:T(8,128)S(1)}, f32[2,4,72,128]{3,2,1,0:T(8,128)S(1)}, u32[]{:S(2)}, u32[]{:S(2)}) collective-permute-start(f32[2,4,72,128]{3,2,1,0:T(8,128)S(1)} %fusion.2), channel_id=1, source_target_pairs={{0,16},{4,20},{8,24},{12,28},{16,0},{20,4},{24,8},{28,12},{1,17},{... | collective-permute-start | bytes 884744 | tf_op jit(solution)/shard_map/ppermute | solution.py:221
  95.1 2.6 %collective-permute-start.9 = (f32[1,4,72,128]{3,2,1,0:T(8,128)S(1)}, f32[1,4,72,128]{3,2,1,0:T(8,128)S(1)}, u32[]{:S(2)}, u32[]{:S(2)}) collective-permute-start(f32[1,4,72,128]{3,2,1,0:T(8,128)S(1)} %get-tuple-element.49), channel_id=1, source_target_pairs={{0,16},{4,20},{8,24},{12,28},{16,0},{20,4},{24,8},{28,12},{1,17},{... | collective-permute-start | bytes 442376 | tf_op jit(solution)/shard_map/ppermute | solution.py:221
  97.7 9.1 %collective-permute-done.18 = f32[2,4,72,128]{3,2,1,0:T(8,128)S(1)} collective-permute-done((f32[2,4,72,128]{3,2,1,0:T(8,128)S(1)}, f32[2,4,72,128]{3,2,1,0:T(8,128)S(1)}, u32[]{:S(2)}, u32[]{:S(2)}) %collective-permute-start.18) | collective-permute-done | bytes 294944 | tf_op jit(solution)/shard_map/ppermute | solution.py:221
  108.4 3.0 %collective-permute-start.14 = (f32[1,4,64,128]{3,2,1,0:T(8,128)S(1)}, f32[1,4,64,128]{3,2,1,0:T(8,128)S(1)}, u32[]{:S(2)}, u32[]{:S(2)}) collective-permute-start(f32[1,4,64,128]{3,2,1,0:T(8,128)S(1)} %get-tuple-element.51), channel_id=1, source_target_pairs={{0,16},{4,20},{8,24},{12,28},{16,0},{20,4},{24,8},{28,12},{1,17},{... | collective-permute-start | bytes 393224 | tf_op jit(solution)/shard_map/ppermute | solution.py:221
  111.5 12.7 %collective-permute-done.14 = f32[1,4,64,128]{3,2,1,0:T(8,128)S(1)} collective-permute-done((f32[1,4,64,128]{3,2,1,0:T(8,128)S(1)}, f32[1,4,64,128]{3,2,1,0:T(8,128)S(1)}, u32[]{:S(2)}, u32[]{:S(2)}) %collective-permute-start.14) | collective-permute-done | bytes 131104 | tf_op jit(solution)/shard_map/ppermute | solution.py:221
  124.2 2.0 %finish.1 = f32[4,3,96,128]{3,2,1,0:T(8,128)} custom-call(f32[4,96,9]{2,1,0:T(8,128)S(1)} %copy.20.tangent_ref, f32[4,80,128]{2,1,0:T(8,128)S(1)} %get-tuple-element.46.rest_0_, f32[4,80,128]{2,1,0:T(8,128)S(1)} %bitcast.110, f32[4,72,128]{2,1,0:T(8,128)S(1)} %get-tuple-element.50.rest_2_, f32[4,72,128]{2,1,0:T(8,128)S(1)} %bitcast.111, ...), custom_call_target="tpu_custom_call" | custom-call | flops 884736 | bytes 2359296 | tf_op jit(solution)/shard_map/finish/pallas_call | solution.py:189
  (74 shorter events, 19.7 us)
Async XLA Ops:
  0.0 14.9 %copy-start.15 = (s32[24]{0:T(128)S(1)}, s32[24]{0:T(128)}, u32[]{:S(2)}) copy-start(s32[24]{0:T(128)} %param.10) | copy-start | bytes 292
  0.0 14.9 %copy-start.16 = (s32[24,1]{0,1:T(1,128)S(1)}, s32[24,1]{0,1:T(1,128)}, u32[]{:S(2)}) copy-start(s32[24,1]{0,1:T(1,128)} %param.9) | copy-start | bytes 292
  13.9 3.9 %collective-permute-start.5 = (f32[2,24,72,128]{3,2,1,0:T(8,128)}, f32[2,24,72,128]{3,2,1,0:T(8,128)S(1)}, u32[]{:S(2)}, u32[]{:S(2)}) collective-permute-start(f32[2,24,72,128]{3,2,1,0:T(8,128)} %get-tuple-element.26), channel_id=1, source_target_pairs={{0,1},{1,0},{2,3},{3,2},{4,5},{5,4},{6,7},{7,6},{8,9},{9,8},{10,11... | collective-permute-start | bytes 5308424 | tf_op jit(solution)/shard_map/ppermute | solution.py:221
  13.9 12.9 %collective-permute-start.15 = (f32[2,24,72,128]{3,2,1,0:T(8,128)}, f32[2,24,72,128]{3,2,1,0:T(8,128)S(1)}, u32[]{:S(2)}, u32[]{:S(2)}) collective-permute-start(f32[2,24,72,128]{3,2,1,0:T(8,128)} %get-tuple-element.34), channel_id=1, source_target_pairs={{0,1},{1,0},{2,3},{3,2},{4,5},{5,4},{6,7},{7,6},{8,9},{9,8},{10,11... | collective-permute-start | bytes 5308424 | tf_op jit(solution)/shard_map/ppermute | solution.py:221
  14.4 18.3 %collective-permute-start = (f32[2,24,80,128]{3,2,1,0:T(8,128)}, f32[2,24,80,128]{3,2,1,0:T(8,128)}, u32[]{:S(2)}, u32[]{:S(2)}) collective-permute-start(f32[2,24,80,128]{3,2,1,0:T(8,128)} %get-tuple-element.22), channel_id=1, source_target_pairs={{0,1},{1,0},{2,3},{3,2},{4,5},{5,4},{6,7},{7,6},{8,9},{9,8},{10,11... | collective-permute-start | bytes 5898248 | tf_op jit(solution)/shard_map/ppermute | solution.py:221
  14.5 15.9 %collective-permute-start.10 = (f32[2,24,64,128]{3,2,1,0:T(8,128)}, f32[2,24,64,128]{3,2,1,0:T(8,128)}, u32[]{:S(2)}, u32[]{:S(2)}) collective-permute-start(f32[2,24,64,128]{3,2,1,0:T(8,128)} %get-tuple-element.30), channel_id=1, source_target_pairs={{0,1},{1,0},{2,3},{3,2},{4,5},{5,4},{6,7},{7,6},{8,9},{9,8},{10,11... | collective-permute-start | bytes 4718600 | tf_op jit(solution)/shard_map/ppermute | solution.py:221
  25.2 31.4 %collective-permute-start.6 = (f32[2,16,72,128]{3,2,1,0:T(8,128)}, f32[2,16,72,128]{3,2,1,0:T(8,128)}, u32[]{:S(2)}, u32[]{:S(2)}) collective-permute-start(f32[2,16,72,128]{3,2,1,0:T(8,128)} %get-tuple-element.28), channel_id=1, source_target_pairs={{0,8},{4,12},{8,0},{12,4},{16,24},{20,28},{24,16},{28,20},{1,9},{5... | collective-permute-start | bytes 3538952 | tf_op jit(solution)/shard_map/ppermute | solution.py:221
  29.8 29.8 %collective-permute-start.16 = (f32[2,16,72,128]{3,2,1,0:T(8,128)}, f32[2,16,72,128]{3,2,1,0:T(8,128)}, u32[]{:S(2)}, u32[]{:S(2)}) collective-permute-start(f32[2,16,72,128]{3,2,1,0:T(8,128)} %get-tuple-element.36), channel_id=1, source_target_pairs={{0,4},{4,0},{8,12},{12,8},{16,20},{20,16},{24,28},{28,24},{1,5},{5... | collective-permute-start | bytes 3538952 | tf_op jit(solution)/shard_map/ppermute | solution.py:221
  32.2 20.5 %collective-permute-start.11 = (f32[1,24,64,128]{3,2,1,0:T(8,128)S(1)}, f32[1,24,64,128]{3,2,1,0:T(8,128)S(1)}, u32[]{:S(2)}, u32[]{:S(2)}) collective-permute-start(f32[1,24,64,128]{3,2,1,0:T(8,128)S(1)} %get-tuple-element.39), channel_id=1, source_target_pairs={{0,2},{1,3},{2,0},{3,1},{4,6},{5,7},{6,4},{7,5},{8,10},{9,11},{10,... | collective-permute-start | bytes 2359304 | tf_op jit(solution)/shard_map/ppermute | solution.py:221
  35.4 21.1 %copy-start.5 = (f32[2,16,72,128]{3,2,1,0:T(8,128)S(1)}, f32[2,16,72,128]{3,2,1,0:T(8,128)}, u32[]{:S(2)}) copy-start(f32[2,16,72,128]{3,2,1,0:T(8,128)} %copy-done.4) | copy-start | bytes 3538948
  35.4 38.3 %collective-permute-start.1 = (f32[1,24,80,128]{3,2,1,0:T(8,128)}, f32[1,24,80,128]{3,2,1,0:T(8,128)S(1)}, u32[]{:S(2)}, u32[]{:S(2)}) collective-permute-start(f32[1,24,80,128]{3,2,1,0:T(8,128)} %get-tuple-element.37), channel_id=1, source_target_pairs={{0,2},{1,3},{2,0},{3,1},{4,6},{5,7},{6,4},{7,5},{8,10},{9,11},{10,... | collective-permute-start | bytes 2949128 | tf_op jit(solution)/shard_map/ppermute | solution.py:221
  55.1 21.1 %collective-permute-start.12 = (f32[1,16,64,128]{3,2,1,0:T(8,128)}, f32[1,16,64,128]{3,2,1,0:T(8,128)}, u32[]{:S(2)}, u32[]{:S(2)}) collective-permute-start(f32[1,16,64,128]{3,2,1,0:T(8,128)} %get-tuple-element.32), channel_id=1, source_target_pairs={{0,4},{4,0},{8,12},{12,8},{16,20},{20,16},{24,28},{28,24},{1,5},{5... | collective-permute-start | bytes 1572872 | tf_op jit(solution)/shard_map/ppermute | solution.py:221
  59.1 26.0 %collective-permute-start.7 = (f32[1,16,72,128]{3,2,1,0:T(8,128)}, f32[1,16,72,128]{3,2,1,0:T(8,128)}, u32[]{:S(2)}, u32[]{:S(2)}) collective-permute-start(f32[1,16,72,128]{3,2,1,0:T(8,128)} %get-tuple-element.44), channel_id=1, source_target_pairs={{0,2},{1,3},{2,0},{3,1},{4,6},{5,7},{6,4},{7,5},{8,10},{9,11},{10,... | collective-permute-start | bytes 1769480 | tf_op jit(solution)/shard_map/ppermute | solution.py:221
  62.0 26.6 %collective-permute-start.17 = (f32[4,4,72,128]{3,2,1,0:T(8,128)}, f32[4,4,72,128]{3,2,1,0:T(8,128)}, u32[]{:S(2)}, u32[]{:S(2)}) collective-permute-start(f32[4,4,72,128]{3,2,1,0:T(8,128)} %get-tuple-element.42), channel_id=1, source_target_pairs={{0,8},{4,12},{8,0},{12,4},{16,24},{20,28},{24,16},{28,20},{1,9},{5... | collective-permute-start | bytes 1769480 | tf_op jit(solution)/shard_map/ppermute | solution.py:221
  74.6 18.7 %collective-permute-start.2 = (f32[1,16,80,128]{3,2,1,0:T(8,128)S(1)}, f32[1,16,80,128]{3,2,1,0:T(8,128)S(1)}, u32[]{:S(2)}, u32[]{:S(2)}) collective-permute-start(f32[1,16,80,128]{3,2,1,0:T(8,128)S(1)} %get-tuple-element.24), channel_id=1, source_target_pairs={{0,4},{4,0},{8,12},{12,8},{16,20},{20,16},{24,28},{28,24},{1,5},{5... | collective-permute-start | bytes 1966088 | tf_op jit(solution)/shard_map/ppermute | solution.py:221
  77.2 31.1 %collective-permute-start.13 = (f32[2,4,64,128]{3,2,1,0:T(8,128)S(1)}, f32[2,4,64,128]{3,2,1,0:T(8,128)S(1)}, u32[]{:S(2)}, u32[]{:S(2)}) collective-permute-start(f32[2,4,64,128]{3,2,1,0:T(8,128)S(1)} %fusion.4), channel_id=1, source_target_pairs={{0,8},{4,12},{8,0},{12,4},{16,24},{20,28},{24,16},{28,20},{1,9},{5... | collective-permute-start | bytes 786440 | tf_op jit(solution)/shard_map/ppermute | solution.py:221
  86.1 9.0 %collective-permute-start.8 = (f32[2,4,72,128]{3,2,1,0:T(8,128)S(1)}, f32[2,4,72,128]{3,2,1,0:T(8,128)S(1)}, u32[]{:S(2)}, u32[]{:S(2)}) collective-permute-start(f32[2,4,72,128]{3,2,1,0:T(8,128)S(1)} %fusion.3), channel_id=1, source_target_pairs={{0,4},{4,0},{8,12},{12,8},{16,20},{20,16},{24,28},{28,24},{1,5},{5... | collective-permute-start | bytes 884744 | tf_op jit(solution)/shard_map/ppermute | solution.py:221
  90.7 16.2 %collective-permute-start.18 = (f32[2,4,72,128]{3,2,1,0:T(8,128)S(1)}, f32[2,4,72,128]{3,2,1,0:T(8,128)S(1)}, u32[]{:S(2)}, u32[]{:S(2)}) collective-permute-start(f32[2,4,72,128]{3,2,1,0:T(8,128)S(1)} %fusion.2), channel_id=1, source_target_pairs={{0,16},{4,20},{8,24},{12,28},{16,0},{20,4},{24,8},{28,12},{1,17},{... | collective-permute-start | bytes 884744 | tf_op jit(solution)/shard_map/ppermute | solution.py:221
  93.4 14.9 %collective-permute-start.3 = (f32[2,4,80,128]{3,2,1,0:T(8,128)S(1)}, f32[2,4,80,128]{3,2,1,0:T(8,128)S(1)}, u32[]{:S(2)}, u32[]{:S(2)}) collective-permute-start(f32[2,4,80,128]{3,2,1,0:T(8,128)S(1)} %fusion.1), channel_id=1, source_target_pairs={{0,8},{4,12},{8,0},{12,4},{16,24},{20,28},{24,16},{28,20},{1,9},{5... | collective-permute-start | bytes 983048 | tf_op jit(solution)/shard_map/ppermute | solution.py:221
  93.9 17.4 %copy-start.14 = (f32[4,3,3,96]{3,0,2,1:T(4,128)S(1)}, f32[4,3,3,96]{3,0,2,1:T(4,128)}, u32[]{:S(2)}) copy-start(f32[4,3,3,96]{3,0,2,1:T(4,128)} %param.11) | copy-start | bytes 41476
  95.1 29.1 %collective-permute-start.9 = (f32[1,4,72,128]{3,2,1,0:T(8,128)S(1)}, f32[1,4,72,128]{3,2,1,0:T(8,128)S(1)}, u32[]{:S(2)}, u32[]{:S(2)}) collective-permute-start(f32[1,4,72,128]{3,2,1,0:T(8,128)S(1)} %get-tuple-element.49), channel_id=1, source_target_pairs={{0,16},{4,20},{8,24},{12,28},{16,0},{20,4},{24,8},{28,12},{1,17},{... | collective-permute-start | bytes 442376 | tf_op jit(solution)/shard_map/ppermute | solution.py:221
  106.9 17.2 %collective-permute-start.19 = (f32[1,4,72,128]{3,2,1,0:T(8,128)S(1)}, f32[1,4,72,128]{3,2,1,0:T(8,128)S(1)}, u32[]{:S(2)}, u32[]{:S(2)}) collective-permute-start(f32[1,4,72,128]{3,2,1,0:T(8,128)S(1)} %get-tuple-element.47), channel_id=1, source_target_pairs={{0,2},{1,3},{2,0},{3,1},{4,6},{5,7},{6,4},{7,5},{8,10},{9,11},{10,... | collective-permute-start | bytes 442376 | tf_op jit(solution)/shard_map/ppermute | solution.py:221
  108.3 15.9 %collective-permute-start.4 = (f32[1,4,80,128]{3,2,1,0:T(8,128)S(1)}, f32[1,4,80,128]{3,2,1,0:T(8,128)S(1)}, u32[]{:S(2)}, u32[]{:S(2)}) collective-permute-start(f32[1,4,80,128]{3,2,1,0:T(8,128)S(1)} %get-tuple-element.45), channel_id=1, source_target_pairs={{0,16},{4,20},{8,24},{12,28},{16,0},{20,4},{24,8},{28,12},{1,17},{... | collective-permute-start | bytes 491528 | tf_op jit(solution)/shard_map/ppermute | solution.py:221
  108.4 15.8 %collective-permute-start.14 = (f32[1,4,64,128]{3,2,1,0:T(8,128)S(1)}, f32[1,4,64,128]{3,2,1,0:T(8,128)S(1)}, u32[]{:S(2)}, u32[]{:S(2)}) collective-permute-start(f32[1,4,64,128]{3,2,1,0:T(8,128)S(1)} %get-tuple-element.51), channel_id=1, source_target_pairs={{0,16},{4,20},{8,24},{12,28},{16,0},{20,4},{24,8},{28,12},{1,17},{... | collective-permute-start | bytes 393224 | tf_op jit(solution)/shard_map/ppermute | solution.py:221
  (13 other events, 58.9 us)
